TPU v7x, 256 devices: a whole 4x4x8 slice. The times are simulated.
256 devices in a mesh: buf: 32 (over x, y, core), lat: 8 (over z).
Axes of the slice: x: 4, y: 4, z: 8, core: 2. Of those that a mesh axis runs over, the one named last changes fastest.
Arguments:
- buffer: bfloat16 [8192, 4096], P('buf'), may hold values from -6 to 6
- sample_rows: int32 [8192], P('lat'), may hold values from 0 to 8191, as said below
- window: bfloat16 [24576, 4096], P('buf'), may hold values from -6 to 6
- enc_scale: float32 [8192], P('lat'), may hold values from 0.5 to 2
- dec_bias: float32 [4096], replicated, may hold values from -3 to 3
Outputs:
- recon: bfloat16 [24576, 4096], P('buf', 'lat')
Inputs may be any that keep to these rules, and one draw needn't show every extreme that they name: `sample_rows`: entry k names the buffer row sampled for reseeded latent k; shard s of the buffer holds rows s * 256 to (s + 1) * 256 - 1. In each aligned block of 32 entries at most 2 name rows of one shard, and in every block some shard gives exactly 2. In each owner's 1024 entries at most 64 name rows of one shard, and some shard gives exactly 64.
All inputs are finite; a program needn't handle non-finite values.
Results may differ from a plain program's by a relative error of at most 0.018.
Values may be sent and summed in bfloat16 or wider, within the bound.
A program may use at most 128 MiB of HBM per device.

v0:
```python
import jax
import jax.numpy as jnp
from jax import lax
from jax.sharding import PartitionSpec as P


def unit_rows(picked_rows):
    values = picked_rows.astype(jnp.float32)
    squares = jnp.sum(values * values, axis=1, keepdims=True)
    return (values * lax.rsqrt(squares + 1e-06)).astype(jnp.bfloat16)


def encode_block(centered, unit_block, scale_block):
    scores = lax.dot_general(
        centered, unit_block, (((1,), (1,)), ((), ())), preferred_element_type=jnp.float32
    )
    return jnp.maximum(scores * scale_block[None, :], 0.0).astype(jnp.bfloat16)


def pick_units(buffer, pick_index):
    picked = jnp.take(buffer, jnp.maximum(pick_index, 0), axis=0)
    picked = jnp.where((pick_index >= 0)[:, None], picked, jnp.zeros_like(picked))
    return unit_rows(picked)


def on_device(buffer, sample_rows, window, enc_scale, dec_bias):
    shard_count = lax.axis_size("buf")
    shard_index = lax.axis_index("buf")
    owner_count = sample_rows.shape[0]
    slot_count = owner_count // shard_count
    shard_rows = buffer.shape[0]
    capacity = 2 + (slot_count - 1) // shard_count
    source = sample_rows // shard_rows
    offset = sample_rows - source * shard_rows
    centered = (window.astype(jnp.float32) - dec_bias[None, :]).astype(jnp.bfloat16)
    positions = jnp.arange(owner_count, dtype=jnp.int32)
    own_capacity = shard_count * capacity
    matching = source[:, None] == source[None, :]
    earlier = positions[:, None] < positions[None, :]
    owner_rank = jnp.sum((matching & earlier).astype(jnp.int32), axis=0)
    room_iota = jnp.arange(own_capacity, dtype=jnp.int32)
    chosen = (source == shard_index)[:, None] & (owner_rank[:, None] == room_iota[None, :])
    pick_index = jnp.sum(jnp.where(chosen, offset[:, None] + 1, 0), axis=0) - 1
    packed = pick_units(buffer, pick_index)
    collected = lax.all_gather(packed, "buf", axis=0, tiled=True)
    all_units = jnp.take(collected, source * own_capacity + owner_rank, axis=0)
    active_all = encode_block(centered, all_units, enc_scale)
    partial_value = jnp.dot(active_all, all_units, preferred_element_type=jnp.float32)
    rounded = partial_value.astype(jnp.bfloat16).astype(jnp.float32)
    summed = lax.psum_scatter(
        rounded.astype(jnp.bfloat16), "lat", scatter_dimension=1, tiled=True
    ).astype(jnp.float32)
    feature_count = summed.shape[1]
    bias_part = lax.dynamic_slice_in_dim(
        dec_bias, lax.axis_index("lat") * feature_count, feature_count
    )
    return (summed + bias_part[None, :]).astype(jnp.bfloat16)


def solution(mesh):
    in_specs = (P("buf", None), P("lat"), P("buf", None), P("lat"), P())
    out_specs = P("buf", "lat")
    return jax.shard_map(
        on_device, mesh=mesh, in_specs=in_specs, out_specs=out_specs, check_vma=False
    )
```

profile of v0, /device:TPU:1, one launch (start us, length us, event | category | flops | bytes accessed | tf_op | source)
XLA Modules:
  0.0 220.5 jit_solution(11854953599494018754)
XLA Ops:
  6.5 0.0 copy-start
  6.5 0.0 all-gather.2.cloned.1.call-start
  6.5 0.8 add_select_fusion
  7.4 0.4 convert_reduce_fusion
  7.8 0.7 broadcast_clamp_fusion
  8.5 0.7 compare_and_fusion
  9.2 0.2 select_reduce_fusion
  9.4 0.0 copy-done
  9.4 0.9 gather_fusion
  10.3 0.3 fusion.3
  10.6 1.0 fusion.4
  11.7 0.0 all-gather.2.cloned.1.call-update
  11.7 0.0 reduce-scatter.2.cloned.1.call-start
  11.7 81.8 %all-gather.2.cloned.1.call-done = bf16[2048,4096]{1,0:T(8,128)(2,1)} async-done(((bf16[64,4096]{1,0:T(8,128)(2,1)}), bf16[2048,4096]{1,0:T(8,128)(2,1)}) %all-gather.2.cloned.1.call-update) | async-done | bytes 16777232 | tf_op jit(solution)/shard_map/all_gather | solution.py:45
  93.6 0.0 copy-start.2
  93.6 0.0 copy-start.3
  93.6 23.0 %gather_fusion.1 = bf16[1024,4096]{1,0:T(8,128)(2,1)} fusion(bf16[2048,4096]{1,0:T(8,128)(2,1)} %all-gather.2.cloned.1.call-done, s32[1024]{0:T(1024)S(1)} %get-tuple-element.7), kind=kCustom, calls=%fused_computation.1 | custom fusion | bytes 16781312 | tf_op jit(solution)/shard_map/jit(_take)/gather | solution.py:46
  116.6 0.0 copy-done.2
  116.6 0.0 copy-done.3
  116.6 0.0 copy-start.1
  116.6 11.6 %maximum_convert_fusion = bf16[768,1024]{1,0:T(8,128)(2,1)S(1)} fusion(bf16[1024,4096]{1,0:T(8,128)(2,1)} %gather_fusion.1, pred[1024]{0:T(1024)(128)(4,1)S(1)} %get-tuple-element.5, bf16[768,4096]{1,0:T(8,128)(2,1)} %param.7, f32[4096]{0:T(1024)S(1)} %copy-done.2, f32[1024]{0:T(1024)S(1)} %copy-done.3), kind=kOutput, calls=%fused_computation.10 | convolution fusion | flops 6458441728 | bytes 16274432 | tf_op jit(solution)/shard_map/dot_general | solution.py:14
  128.3 0.0 copy-done.1
  128.3 8.8 %convolution_convert_fusion = bf16[768,4096]{1,0:T(8,128)(2,1)} fusion(bf16[768,1024]{1,0:T(8,128)(2,1)S(1)} %maximum_convert_fusion, bf16[1024,4096]{1,0:T(8,128)(2,1)S(1)} %copy-done.1, pred[1024]{0:T(1024)(128)(4,1)S(1)} %get-tuple-element.5), kind=kOutput, calls=%fused_computation.4 | convolution fusion | flops 6449790976 | bytes 16253952 | tf_op jit(solution)/shard_map/dot_general | solution.py:48
  137.1 0.0 reduce-scatter.2.cloned.1.call-update
  137.1 0.1 dynamic_slice.3
  137.2 74.4 %reduce-scatter.2.cloned.1.call-done = bf16[768,512]{1,0:T(8,128)(2,1)} async-done(((bf16[768,4096]{1,0:T(8,128)(2,1)}), bf16[768,512]{1,0:T(8,128)(2,1)}) %reduce-scatter.2.cloned.1.call-update) | async-done | bytes 786448 | tf_op jit(solution)/shard_map/reduce_scatter | solution.py:50
  211.5 2.2 add_convert_fusion
  (4 shorter events, 0.0 us)
Async XLA Ops:
  6.5 2.9 %copy-start = (bf16[256,4096]{1,0:T(8,128)(2,1)S(1)}, bf16[256,4096]{1,0:T(8,128)(2,1)}, u32[]{:S(2)}) copy-start(bf16[256,4096]{1,0:T(8,128)(2,1)} %param.5) | copy-start | bytes 6291460
  6.5 87.0 %all-gather.2.cloned.1.call-start = ((), (), s32[]{:S(2)}) async-start(), calls=%async_computation.1 | async-start | bytes 17301504 | tf_op jit(solution)/shard_map/all_gather | solution.py:45
  11.7 199.9 %reduce-scatter.2.cloned.1.call-start = ((), (), s32[]{:S(2)}) async-start(), calls=%async_computation.2 | async-start | bytes 7077888 | tf_op jit(solution)/shard_map/reduce_scatter | solution.py:50
  93.6 23.0 %copy-start.2 = (f32[4096]{0:T(1024)S(1)}, f32[4096]{0:T(1024)}, u32[]{:S(2)}) copy-start(f32[4096]{0:T(1024)} %param.9) | copy-start | bytes 49156
  93.6 23.0 %copy-start.3 = (f32[1024]{0:T(1024)S(1)}, f32[1024]{0:T(1024)}, u32[]{:S(2)}) copy-start(f32[1024]{0:T(1024)} %param.8) | copy-start | bytes 12292
  116.6 11.7 %copy-start.1 = (bf16[1024,4096]{1,0:T(8,128)(2,1)S(1)}, bf16[1024,4096]{1,0:T(8,128)(2,1)}, u32[]{:S(2)}) copy-start(bf16[1024,4096]{1,0:T(8,128)(2,1)} %gather_fusion.1) | copy-start | bytes 25165828
Sparse Core Ops, SparseCore 0:
  11.8 81.7 all-gather.1
  137.2 74.2 reduce-scatter.1
where the time goes:
time: 221 us
  waiting for transfers between devices  156 us (71%)
  local copies, waits for them, and re-layouts  24 us (11%)
  matrix products  20.4 us (9%)
  between operations  13.5 us (6%)
  other arithmetic  6.37 us (3%)
    all_gather x1, waiting for transfers between devices, on_device(): collected = lax.all_gather(packed, 'buf', axis=0, tiled=True)  81.8 us
    reduce_scatter x1, waiting for transfers between devices, on_device(): lax.psum_scatter(rounded.astype(jnp.bfloat16), 'lat', scatter_dimension=1...  74.4 us
    gather x1, local copies, waits for them, and re-layouts, on_device(): all_units = jnp.take(collected, source * own_capacity + owner_rank, axis=0)  23 us
    dot_general x1, matrix products, encode_block(): lax.dot_general(centered, unit_block, (((1,), (1,)), ((), ())), preferred...  11.6 us
    dot_general x1, matrix products, on_device(): jnp.dot(active_all, all_units, preferred_element_type=jnp.float32)  8.79 us
  transfers between devices with their start and end apart: 2, of which 2 were waited for; matrix products, arithmetic and copies ran while one was open for 0% of the time, Pallas kernels for 0%

commit v1 on v0

--- a/solution.py
+++ b/solution.py
@@ -2,6 +2,18 @@
 import jax.numpy as jnp
 from jax import lax
 from jax.sharding import PartitionSpec as P
+
+
+def gather_by_bits(array, axis, dim):
+    ways, here = (lax.axis_size(axis), lax.axis_index(axis))
+    grown, reach = (array, 1)
+    while reach < ways:
+        theirs = lax.ppermute(grown, axis, [(d, d ^ reach) for d in range(ways)])
+        mine_first = jnp.concatenate([grown, theirs], axis=dim)
+        theirs_first = jnp.concatenate([theirs, grown], axis=dim)
+        grown = jnp.where(here & reach == 0, mine_first, theirs_first)
+        reach = 2 * reach
+    return grown
 
 
 def unit_rows(picked_rows):
@@ -42,7 +54,7 @@
     chosen = (source == shard_index)[:, None] & (owner_rank[:, None] == room_iota[None, :])
     pick_index = jnp.sum(jnp.where(chosen, offset[:, None] + 1, 0), axis=0) - 1
     packed = pick_units(buffer, pick_index)
-    collected = lax.all_gather(packed, "buf", axis=0, tiled=True)
+    collected = gather_by_bits(packed, "buf", 0)
     all_units = jnp.take(collected, source * own_capacity + owner_rank, axis=0)
     active_all = encode_block(centered, all_units, enc_scale)
     partial_value = jnp.dot(active_all, all_units, preferred_element_type=jnp.float32)

time: 221 us -> 529 us (2.39)
  waiting for transfers between devices: 156 us -> 422 us
  other arithmetic: 6.37 us -> 43.1 us
  starting transfers between devices: 0.04 us -> 5.7 us
    ppermute x0 -> x5, waiting for transfers between devices: none -> 342 us  [gather_by_bits(): theirs = lax.ppermute(grown, axis, [(d, d ^ reach) for d in range(ways)])]
    all_gather x1 -> x0, waiting for transfers between devices: 81.8 us -> none  [on_device(): collected = lax.all_gather(packed, 'buf', axis=0, tiled=True)]
    select_n x0 -> x5, other arithmetic: none -> 37.5 us  [gather_by_bits(): grown = jnp.where(here & reach == 0, mine_first, theirs_first)]
    ppermute x0 -> x5, starting transfers between devices: none -> 5.7 us  [gather_by_bits(): theirs = lax.ppermute(grown, axis, [(d, d ^ reach) for d in range(ways)])]
    reduce_scatter x1, waiting for transfers between devices: 74.4 us -> 79.8 us  [on_device(): lax.psum_scatter(rounded.astype(jnp.bfloat16), 'lat', scatter_dimension=1...]
  transfers between devices with their start and end apart: 2 -> 6, of which waited for: 2 -> 6; matrix products, arithmetic and copies ran while one was open for 0% -> 0% of each run, Pallas kernels for 0% -> 0%
where the time goes in v1:
time: 529 us
  waiting for transfers between devices  422 us (80%)
  other arithmetic  43.1 us (8%)
  local copies, waits for them, and re-layouts  24 us (5%)
  matrix products  20.6 us (4%)
  between operations  13.5 us (3%)
  starting transfers between devices  5.7 us (1%)
    ppermute x5, waiting for transfers between devices, gather_by_bits(): theirs = lax.ppermute(grown, axis, [(d, d ^ reach) for d in range(ways)])  342 us
    reduce_scatter x1, waiting for transfers between devices, on_device(): lax.psum_scatter(rounded.astype(jnp.bfloat16), 'lat', scatter_dimension=1...  79.8 us
    select_n x5, other arithmetic, gather_by_bits(): grown = jnp.where(here & reach == 0, mine_first, theirs_first)  37.5 us
    gather x1, local copies, waits for them, and re-layouts, on_device(): all_units = jnp.take(collected, source * own_capacity + owner_rank, axis=0)  23 us
    dot_general x1, matrix products, encode_block(): lax.dot_general(centered, unit_block, (((1,), (1,)), ((), ())), preferred...  11.6 us
  transfers between devices with their start and end apart: 6, of which 6 were waited for; matrix products, arithmetic and copies ran while one was open for 0% of the time, Pallas kernels for 0%

profile of v1, /device:TPU:1, one launch (start us, length us, event | category | flops | bytes accessed | tf_op | source)
XLA Modules:
  0.0 528.9 jit_solution(11258948766792162898)
XLA Ops:
  6.5 0.0 copy-start
  6.5 0.0 reduce-scatter.2.cloned.1.call-start
  6.5 0.8 add_select_fusion
  7.4 0.4 convert_reduce_fusion
  7.8 0.7 broadcast_clamp_fusion
  8.5 0.7 compare_and_fusion
  9.2 0.2 select_reduce_fusion
  9.4 0.0 copy-done
  9.4 0.9 gather_fusion
  10.3 0.3 fusion.3
  10.6 0.2 fusion.4
  10.9 3.3 collective-permute-start
  14.2 1.5 collective-permute-done
  15.7 0.2 maximum_select_fusion.4
  16.0 0.1 collective-permute-start.1
  16.1 24.5 %collective-permute-done.1 = bf16[128,4096]{1,0:T(8,128)(2,1)} collective-permute-done((bf16[128,4096]{1,0:T(8,128)(2,1)S(1)}, bf16[128,4096]{1,0:T(8,128)(2,1)}, u32[]{:S(2)}, u32[]{:S(2)}) %collective-permute-start.1) | collective-permute-done | bytes 1048608 | tf_op jit(solution)/shard_map/ppermute | solution.py:11
  40.5 2.3 maximum_select_fusion.3
  42.8 1.3 collective-permute-start.2
  44.1 46.4 %collective-permute-done.2 = bf16[256,4096]{1,0:T(8,128)(2,1)} collective-permute-done((bf16[256,4096]{1,0:T(8,128)(2,1)S(1)}, bf16[256,4096]{1,0:T(8,128)(2,1)}, u32[]{:S(2)}, u32[]{:S(2)}) %collective-permute-start.2) | collective-permute-done | bytes 2097184 | tf_op jit(solution)/shard_map/ppermute | solution.py:11
  90.4 5.1 maximum_select_fusion.2
  95.6 0.0 collective-permute-start.3
  95.6 90.3 %collective-permute-done.3 = bf16[512,4096]{1,0:T(8,128)(2,1)} collective-permute-done((bf16[512,4096]{1,0:T(8,128)(2,1)}, bf16[512,4096]{1,0:T(8,128)(2,1)}, u32[]{:S(2)}, u32[]{:S(2)}) %collective-permute-start.3) | collective-permute-done | bytes 4194336 | tf_op jit(solution)/shard_map/ppermute | solution.py:11
  185.8 11.1 %maximum_select_fusion.1 = bf16[1024,4096]{1,0:T(8,128)(2,1)} fusion(bf16[512,4096]{1,0:T(8,128)(2,1)} %collective-permute-done.3, bf16[512,4096]{1,0:T(8,128)(2,1)} %maximum_select_fusion.2, pred[]{:T(512)S(6)} %eq.51), kind=kLoop, calls=%fused_computation.4 | loop fusion | flops 37748736 | bytes 16777216 | tf_op jit(solution)/shard_map/jit(_where)/select_n | solution.py:14
  196.9 1.0 collective-permute-start.4
  197.9 179.7 %collective-permute-done.4 = bf16[1024,4096]{1,0:T(8,128)(2,1)} collective-permute-done((bf16[1024,4096]{1,0:T(8,128)(2,1)}, bf16[1024,4096]{1,0:T(8,128)(2,1)}, u32[]{:S(2)}, u32[]{:S(2)}) %collective-permute-start.4) | collective-permute-done | bytes 8388640 | tf_op jit(solution)/shard_map/ppermute | solution.py:11
  377.6 18.8 %maximum_select_fusion = bf16[2048,4096]{1,0:T(8,128)(2,1)} fusion(bf16[1024,4096]{1,0:T(8,128)(2,1)} %collective-permute-done.4, bf16[1024,4096]{1,0:T(8,128)(2,1)} %maximum_select_fusion.1, pred[]{:T(512)S(6)} %eq.50), kind=kLoop, calls=%fused_computation.2 | loop fusion | flops 75497472 | bytes 33554432 | tf_op jit(solution)/shard_map/jit(_where)/select_n | solution.py:14
  396.4 0.0 copy-start.3
  396.4 0.0 copy-start.4
  396.4 23.0 %gather_fusion.1 = bf16[1024,4096]{1,0:T(8,128)(2,1)} fusion(bf16[2048,4096]{1,0:T(8,128)(2,1)} %maximum_select_fusion, s32[1024]{0:T(1024)S(1)} %get-tuple-element.7), kind=kCustom, calls=%fused_computation.1 | custom fusion | bytes 16781312 | tf_op jit(solution)/shard_map/jit(_take)/gather | solution.py:58
  419.4 0.0 copy-done.3
  419.4 0.0 copy-done.4
  419.4 0.0 copy-start.2
  419.5 11.6 %maximum_convert_fusion = bf16[768,1024]{1,0:T(8,128)(2,1)S(1)} fusion(bf16[1024,4096]{1,0:T(8,128)(2,1)} %gather_fusion.1, pred[1024]{0:T(1024)(128)(4,1)S(1)} %get-tuple-element.5, bf16[768,4096]{1,0:T(8,128)(2,1)} %param.7, f32[4096]{0:T(1024)S(1)} %copy-done.3, f32[1024]{0:T(1024)S(1)} %copy-done.4), kind=kOutput, calls=%fused_computation.13 | convolution fusion | flops 6458441728 | bytes 16274432 | tf_op jit(solution)/shard_map/dot_general | solution.py:26
  431.1 0.0 copy-done.2
  431.1 0.0 copy-start.1
  431.1 8.9 %convolution_convert_fusion = bf16[768,4096]{1,0:T(8,128)(2,1)} fusion(bf16[768,1024]{1,0:T(8,128)(2,1)S(1)} %maximum_convert_fusion, bf16[1024,4096]{1,0:T(8,128)(2,1)S(1)} %copy-done.2, pred[1024]{0:T(1024)(128)(4,1)S(1)} %get-tuple-element.5), kind=kOutput, calls=%fused_computation.6 | convolution fusion | flops 6449790976 | bytes 16253952 | tf_op jit(solution)/shard_map/dot_general | solution.py:60
  440.0 0.0 reduce-scatter.2.cloned.1.call-update
  440.1 0.1 dynamic_slice.3
  440.1 79.8 %reduce-scatter.2.cloned.1.call-done = bf16[768,512]{1,0:T(8,128)(2,1)} async-done(((bf16[768,4096]{1,0:T(8,128)(2,1)}), bf16[768,512]{1,0:T(8,128)(2,1)}) %reduce-scatter.2.cloned.1.call-update) | async-done | bytes 786448 | tf_op jit(solution)/shard_map/reduce_scatter | solution.py:62
  519.9 2.2 add_convert_fusion
  522.1 0.0 copy-done.1
  (4 shorter events, 0.0 us)
Async XLA Ops:
  6.5 2.9 copy-start
  6.5 513.4 %reduce-scatter.2.cloned.1.call-start = ((), (), s32[]{:S(2)}) async-start(), calls=%async_computation.1 | async-start | bytes 7077888 | tf_op jit(solution)/shard_map/reduce_scatter | solution.py:62
  10.9 4.9 collective-permute-start
  16.0 24.6 %collective-permute-start.1 = (bf16[128,4096]{1,0:T(8,128)(2,1)S(1)}, bf16[128,4096]{1,0:T(8,128)(2,1)}, u32[]{:S(2)}, u32[]{:S(2)}) collective-permute-start(bf16[128,4096]{1,0:T(8,128)(2,1)S(1)} %maximum_select_fusion.4), channel_id=1, source_target_pairs={{0,16},{8,24},{16,0},{24,8},{32,48},{40,56},{48,32},{56,40},{64,80... | collective-permute-start | bytes 3145736 | tf_op jit(solution)/shard_map/ppermute | solution.py:11
  42.8 47.6 %collective-permute-start.2 = (bf16[256,4096]{1,0:T(8,128)(2,1)S(1)}, bf16[256,4096]{1,0:T(8,128)(2,1)}, u32[]{:S(2)}, u32[]{:S(2)}) collective-permute-start(bf16[256,4096]{1,0:T(8,128)(2,1)S(1)} %maximum_select_fusion.3), channel_id=1, source_target_pairs={{0,32},{8,40},{16,48},{24,56},{32,0},{40,8},{48,16},{56,24},{64,96... | collective-permute-start | bytes 6291464 | tf_op jit(solution)/shard_map/ppermute | solution.py:11
  95.6 90.3 %collective-permute-start.3 = (bf16[512,4096]{1,0:T(8,128)(2,1)}, bf16[512,4096]{1,0:T(8,128)(2,1)}, u32[]{:S(2)}, u32[]{:S(2)}) collective-permute-start(bf16[512,4096]{1,0:T(8,128)(2,1)} %maximum_select_fusion.2), channel_id=1, source_target_pairs={{0,64},{8,72},{16,80},{24,88},{32,96},{40,104},{48,112},{56,120},{... | collective-permute-start | bytes 12582920 | tf_op jit(solution)/shard_map/ppermute | solution.py:11
  196.9 180.7 %collective-permute-start.4 = (bf16[1024,4096]{1,0:T(8,128)(2,1)}, bf16[1024,4096]{1,0:T(8,128)(2,1)}, u32[]{:S(2)}, u32[]{:S(2)}) collective-permute-start(bf16[1024,4096]{1,0:T(8,128)(2,1)} %maximum_select_fusion.1), channel_id=1, source_target_pairs={{0,128},{8,136},{16,144},{24,152},{32,160},{40,168},{48,176},{56,1... | collective-permute-start | bytes 25165832 | tf_op jit(solution)/shard_map/ppermute | solution.py:11
  396.4 23.0 %copy-start.3 = (f32[4096]{0:T(1024)S(1)}, f32[4096]{0:T(1024)}, u32[]{:S(2)}) copy-start(f32[4096]{0:T(1024)} %param.9) | copy-start | bytes 49156
  396.4 23.0 %copy-start.4 = (f32[1024]{0:T(1024)S(1)}, f32[1024]{0:T(1024)}, u32[]{:S(2)}) copy-start(f32[1024]{0:T(1024)} %param.8) | copy-start | bytes 12292
  419.4 11.7 %copy-start.2 = (bf16[1024,4096]{1,0:T(8,128)(2,1)S(1)}, bf16[1024,4096]{1,0:T(8,128)(2,1)}, u32[]{:S(2)}) copy-start(bf16[1024,4096]{1,0:T(8,128)(2,1)} %gather_fusion.1) | copy-start | bytes 25165828
  431.1 90.9 %copy-start.1 = (bf16[256,4096]{1,0:T(8,128)(2,1)S(1)}, bf16[256,4096]{1,0:T(8,128)(2,1)}, u32[]{:S(2)}) copy-start(bf16[256,4096]{1,0:T(8,128)(2,1)} %param.5) | copy-start | bytes 6291460
Sparse Core Ops, SparseCore 0:
  440.2 79.6 reduce-scatter.1
